TPU v7x, 32 devices: a whole 2x2x4 slice. The times are simulated.
32 devices in a mesh: tm: 8 (over y, x, core), group: 4 (over z).
Axes of the slice: x: 2, y: 2, z: 4, core: 2. Of those that a mesh axis runs over, the one named last changes fastest.
Arguments:
- frames: bfloat16 [4, 65536, 512], P('group', 'tm')
- pair_count: int32 [4], P('group'), may hold values from 32768 to 63488, as said below
Outputs:
- group_instant: float32 [4, 512, 512], P('group', 'tm')
- group_lagged: float32 [4, 512, 512], P('group', 'tm')
- pooled_instant: float32 [512, 512], P('tm')
- pooled_lagged: float32 [512, 512], P('tm')
Inputs may be any that keep to these rules, and one draw needn't show every extreme that they name: `pair_count`: every session has between 32768 and 63488 pairs, and some session has exactly 63488.
All inputs are finite; a program needn't handle non-finite values.
Results may differ from a plain program's by a relative error of at most 0.0003.
Values may be sent and summed in bfloat16 or wider, within the bound.
A program may use at most 64 MiB of HBM per device.

v0:
```python
import jax
import jax.numpy as jnp
from jax import lax
from jax.sharding import PartitionSpec as P

LAG = 2048


def passed_along(block, axis, distance):
    devices = range(lax.axis_size(axis))
    route = [(i - distance, i) for i in devices if i - distance in devices]
    return lax.ppermute(block, axis, route)


def on_device(frames, pair_count):
    local = frames[0]
    rows = local.shape[0]
    width = local.shape[1]
    share = width // lax.axis_size("tm")
    count = pair_count[0]
    number = count.astype(jnp.float32)
    position = lax.axis_index("tm") * rows + lax.iota(jnp.int32, rows)
    weight = (position < count).astype(jnp.float32)[:, None]
    incoming = passed_along(local[:LAG], "tm", -1)
    lagged = jnp.concatenate([local[LAG:], incoming], axis=0)
    wide = local.astype(jnp.float32)
    later = lagged.astype(jnp.float32)
    sum_x = jnp.sum(wide * weight, axis=0)
    sum_y = jnp.sum(later * weight, axis=0)
    first_row = lax.axis_index("tm") * share
    contract = (((0,), (0,)), ((), ()))
    masked = (wide * weight).astype(jnp.bfloat16)
    raw_inst = lax.dot_general(masked, local, contract, preferred_element_type=jnp.float32)
    raw_lag = lax.dot_general(masked, lagged, contract, preferred_element_type=jnp.float32)
    tot_x, tot_y = lax.psum((sum_x, sum_y), "tm")
    raw_i_rows, raw_l_rows = (
        lax.psum_scatter(raw_inst, "tm", scatter_dimension=0, tiled=True),
        lax.psum_scatter(raw_lag, "tm", scatter_dimension=0, tiled=True),
    )
    mean_x = tot_x / number
    mean_y = tot_y / number
    mean_rows = lax.dynamic_slice_in_dim(mean_x, first_row, share)
    inst_rows = raw_i_rows - number * mean_rows[:, None] * mean_x[None]
    lag_rows = raw_l_rows - number * mean_rows[:, None] * mean_y[None]
    group_instant = (inst_rows / number)[None]
    group_lagged = (lag_rows / number)[None]
    part_inst = inst_rows + number * mean_rows[:, None] * mean_x[None]
    part_lag = lag_rows + number * mean_rows[:, None] * mean_y[None]
    all_inst, all_lag, all_x, all_y, total = lax.psum(
        (part_inst, part_lag, tot_x, tot_y, number.reshape(1)), "group"
    )
    grand = total[0]
    glob_x = all_x / grand
    glob_y = all_y / grand
    glob_rows = lax.dynamic_slice_in_dim(glob_x, first_row, share)
    pooled_instant = (all_inst - grand * glob_rows[:, None] * glob_x[None]) / grand
    pooled_lagged = (all_lag - grand * glob_rows[:, None] * glob_y[None]) / grand
    return (group_instant, group_lagged, pooled_instant, pooled_lagged)


def solution(mesh):
    in_specs = (P("group", "tm", None), P("group"))
    out_specs = (P("group", "tm", None), P("group", "tm", None), P("tm", None), P("tm", None))
    return jax.shard_map(
        on_device, mesh=mesh, in_specs=in_specs, out_specs=out_specs, check_vma=False
    )
```

profile of v0, /device:TPU:0, one launch (start us, length us, event | category | flops | bytes accessed | tf_op | source)
XLA Modules:
  0.0 150.3 jit_solution(18377903120128269848)
XLA Ops:
  7.2 0.0 reduce-scatter.3.cloned.1.call-start
  7.2 3.1 %slice_bitcast_fusion.1 = bf16[2048,512]{1,0:T(8,128)(2,1)} fusion(bf16[1,8192,512]{2,1,0:T(8,128)(2,1)} %param.2), kind=kLoop, calls=%fused_computation.14 | loop fusion | bytes 4194304 | tf_op jit(solution)/shard_map/slice | solution.py:24
  10.3 1.3 collective-permute-start
  12.2 11.5 %fusion.3 = f32[512,512]{1,0:T(8,128)} fusion(bf16[1,8192,512]{2,1,0:T(8,128)(2,1)} %param.2, f32[8192]{0:T(1024)S(1)} %fusion.11), kind=kOutput, calls=%fused_computation.6 | convolution fusion | flops 4307550208 | bytes 9469952 | tf_op jit(solution)/shard_map/dot_general | solution.py:33
  23.8 0.0 reduce-scatter.3.cloned.1.call-update
  23.8 0.0 reduce-scatter.5.cloned.1.call-start
  23.8 3.2 %slice_bitcast_fusion = bf16[6144,512]{1,0:T(8,128)(2,1)S(1)} fusion(bf16[1,8192,512]{2,1,0:T(8,128)(2,1)} %param.2), kind=kLoop, calls=%fused_computation.13 | loop fusion | bytes 12582912 | tf_op jit(solution)/shard_map/slice | solution.py:25
  27.0 0.0 copy-start
  27.0 0.0 collective-permute-done
  27.0 2.6 %copy-done = bf16[6144,512]{1,0:T(8,128)(2,1)} copy-done((bf16[6144,512]{1,0:T(8,128)(2,1)}, bf16[6144,512]{1,0:T(8,128)(2,1)S(1)}, u32[]{:S(2)}) %copy-start) | copy-done | bytes 6291480
  29.7 9.2 %fusion.5 = f32[512,512]{1,0:T(8,128)} fusion(bf16[1,8192,512]{2,1,0:T(8,128)(2,1)} %param.2, f32[8192]{0:T(1024)S(1)} %fusion.11, bf16[2048,512]{1,0:T(8,128)(2,1)S(1)} %collective-permute-done, bf16[6144,512]{1,0:T(8,128)(2,1)S(1)} %slice_bitcast_fusion), kind=kOutput, calls=%fused_computation.7 | convolution fusion | flops 4324327424 | bytes 17858560 | tf_op jit(solution)/shard_map/dot_general | solution.py:34
  38.9 0.0 reduce-scatter.5.cloned.1.call-update
  38.9 0.0 all-reduce.5.cloned.1.call-start
  38.9 9.1 %multiply_reduce_fusion = (f32[512]{0:T(512)S(1)}, f32[512]{0:T(512)S(1)}) fusion(f32[8192]{0:T(1024)S(1)} %fusion.11, bf16[2048,512]{1,0:T(8,128)(2,1)S(1)} %collective-permute-done, bf16[6144,512]{1,0:T(8,128)(2,1)} %copy-done, bf16[1,8192,512]{2,1,0:T(8,128)(2,1)} %param.2), kind=kLoop, calls=%fused_computation | loop fusion | flops 37747712 | bytes 16814080 | tf_op jit(solution)/shard_map/reduce_sum | solution.py:29
  48.0 21.4 %all-reduce = (f32[512]{0:T(512)S(1)}, f32[512]{0:T(512)S(1)}) all-reduce(f32[512]{0:T(512)S(1)} %get-tuple-element.5, f32[512]{0:T(512)S(1)} %get-tuple-element.4), channel_id=1, replica_groups=mesh['tm'=8,'group'=4] {'tm'}, use_global_device_ids=true, to_apply=%region_2.0 | all-reduce | flops 1024 | bytes 8192 | tf_op jit(solution)/shard_map/psum | solution.py:35
  69.4 12.6 %all-reduce.1 = (f32[]{:T(128)}, f32[512]{0:T(512)S(1)}, f32[512]{0:T(512)S(1)}) all-reduce(f32[]{:T(128)S(6)} %convert_element_type.31, f32[512]{0:T(512)S(1)} %get-tuple-element.6, f32[512]{0:T(512)S(1)} %get-tuple-element.7), channel_id=1, replica_groups=mesh['tm'=8,'group'=4] {'group'}, use_global_device_ids=true, to_apply=%region_7.0 | all-reduce | flops 1025 | bytes 8200 | tf_op jit(solution)/shard_map/psum | solution.py:49
  82.1 0.1 dynamic-slice_multiply_fusion.1
  82.2 20.6 %reduce-scatter.5.cloned.1.call-done = f32[64,512]{1,0:T(8,128)} async-done(((f32[512,512]{1,0:T(8,128)}), f32[64,512]{1,0:T(8,128)}) %reduce-scatter.5.cloned.1.call-update) | async-done | bytes 131088 | tf_op jit(solution)/shard_map/reduce_scatter | solution.py:38
  102.7 1.9 %multiply_add_fusion = (f32[64,512]{1,0:T(8,128)}, f32[1,64,512]{2,1,0:T(8,128)}, f32[1,64,512]{2,1,0:T(8,128)}, f32[64,512]{1,0:T(8,128)}) fusion(f32[64,512]{1,0:T(8,128)} %reduce-scatter.5.cloned.1.call-done, f32[512]{0:T(512)S(1)} %get-tuple-element.21, f32[64]{0:T(128)S(1)} %dynamic-slice_multiply_fusion.1, f32[]{:T(128)S(6)} %convert_element_type.31, ...), kind=kLoop, calls=%fused_computation.15 | loop fusion | flops 262144 | bytes 790788 | tf_op jit(solution)/shard_map/add | solution.py:48
  104.6 0.0 all-reduce.5.cloned.1.call-update
  104.6 0.7 broadcast_divide_fusion
  105.3 0.8 dynamic-slice_multiply_fusion
  106.0 35.3 %all-reduce.5.cloned.1.call-done = (f32[64,512]{1,0:T(8,128)}, f32[64,512]{1,0:T(8,128)}) async-done(((f32[64,512]{1,0:T(8,128)}, f32[64,512]{1,0:T(8,128)}), (f32[64,512]{1,0:T(8,128)}, f32[64,512]{1,0:T(8,128)})) %all-reduce.5.cloned.1.call-update) | async-done | bytes 262160 | tf_op jit(solution)/shard_map/psum | solution.py:49
  141.4 2.4 %subtract_divide_fusion = (f32[64,512]{1,0:T(8,128)}, f32[64,512]{1,0:T(8,128)}) fusion(f32[64,512]{1,0:T(8,128)} %get-tuple-element.12, f32[512]{0:T(512)S(1)} %get-tuple-element.23, f32[]{:T(128)} %get-tuple-element.8, f32[64]{0:T(128)S(1)} %dynamic-slice_multiply_fusion, f32[64,512]{1,0:T(8,128)} %get-tuple-element.11, f32[512]{0:T(512)S(1)} %get-tuple-element.24), kind=kLoop, calls=%fused_computation.19 | loop fusion | flops 196608 | bytes 528644 | tf_op jit(solution)/shard_map/div | solution.py:57
  (3 shorter events, 0.0 us)
Async XLA Ops:
  7.2 75.0 %reduce-scatter.3.cloned.1.call-start = ((), (), s32[]{:S(2)}) async-start(), calls=%async_computation.2 | async-start | bytes 1179648 | tf_op jit(solution)/shard_map/reduce_scatter | solution.py:37
  10.3 16.8 %collective-permute-start = (bf16[2048,512]{1,0:T(8,128)(2,1)}, bf16[2048,512]{1,0:T(8,128)(2,1)S(1)}, u32[]{:S(2)}, u32[]{:S(2)}) collective-permute-start(bf16[2048,512]{1,0:T(8,128)(2,1)} %slice_bitcast_fusion.1), channel_id=1, source_target_pairs={{4,0},{8,4},{12,8},{16,12},{20,16},{24,20},{28,24},{5,1},{9,5},{13... | collective-permute-start | bytes 6291464 | tf_op jit(solution)/shard_map/ppermute | solution.py:12
  23.8 78.9 %reduce-scatter.5.cloned.1.call-start = ((), (), s32[]{:S(2)}) async-start(), calls=%async_computation.3 | async-start | bytes 1179648 | tf_op jit(solution)/shard_map/reduce_scatter | solution.py:38
  27.0 2.7 %copy-start = (bf16[6144,512]{1,0:T(8,128)(2,1)}, bf16[6144,512]{1,0:T(8,128)(2,1)S(1)}, u32[]{:S(2)}) copy-start(bf16[6144,512]{1,0:T(8,128)(2,1)S(1)} %slice_bitcast_fusion) | copy-start | bytes 18874372
  38.9 102.5 %all-reduce.5.cloned.1.call-start = ((), (), s32[]{:S(2)}) async-start(), calls=%async_computation.4 | async-start | bytes 524288 | tf_op jit(solution)/shard_map/psum | solution.py:49
Sparse Core Ops, SparseCore 0:
  23.9 39.6 reduce-scatter.2
  66.7 35.9 reduce-scatter.4
  105.7 35.6 all-reduce.4
where the time goes:
time: 151 us; the launch traced here: 150 us
  waiting for transfers between devices  55.9 us (37%)
  blocking collectives  34.1 us (23%)
  matrix products  20.7 us (14%)
  other arithmetic  14.9 us (10%)
  between operations  14.5 us (10%)
  local copies, waits for them, and re-layouts  8.91 us (6%)
    psum x1, waiting for transfers between devices, on_device(): lax.psum((part_inst, part_lag, tot_x, tot_y, number.reshape(1)), 'group')  35.3 us
    psum x1, blocking collectives, on_device(): tot_x, tot_y = lax.psum((sum_x, sum_y), 'tm')  21.4 us
    reduce_scatter x1, waiting for transfers between devices, on_device(): lax.psum_scatter(raw_lag, 'tm', scatter_dimension=0, tiled=True)  20.6 us
    psum x1, blocking collectives, on_device(): lax.psum((part_inst, part_lag, tot_x, tot_y, number.reshape(1)), 'group')  12.6 us
    dot_general x1, matrix products, on_device(): lax.dot_general(masked, local, contract, preferred_element_type=jnp.float32)  11.5 us
    dot_general x1, matrix products, on_device(): lax.dot_general(masked, lagged, contract, preferred_element_type=jnp.floa...  9.18 us
    reduce_sum x1, other arithmetic, on_device(): sum_y = jnp.sum(later * weight, axis=0)  9.06 us
    slice x1, local copies, waits for them, and re-layouts, on_device(): lagged = jnp.concatenate([local[LAG:], incoming], axis=0)  3.19 us
  transfers between devices with their start and end apart: 4, of which 2 were waited for; matrix products, arithmetic and copies ran while one was open for 23% of the time, Pallas kernels for 0%

commit v1 on v0

v1 whole, which is shorter than its diff:
```python
import functools

import jax
import jax.numpy as jnp
from jax import lax
from jax.experimental import pallas as pl
from jax.experimental.pallas import tpu as pltpu
from jax.sharding import PartitionSpec as P

LAG = 2048
MESH = pl.DeviceIdType.MESH
PAD = 16
EXTRA = 8


def kernel(
    T, G, count_ref, frames_ref, gi_ref, gl_ref, pi_ref, po_ref,
    x, xt, head, tail, acc, sx, ai, al, r1i, r1l, r2i, r2l, zi, zl, zri, zrl,
    ld, hs, hr, s1, e1, s2, e2, sz, ez,
):
    F = frames_ref.shape[2]
    R = frames_ref.shape[1]
    H = LAG // 2
    NB = R // H
    S = F // T
    Q = T // 2
    steps = G.bit_length() - 1
    me = lax.axis_index("tm")
    z = lax.axis_index("group")
    c = lax.rem(me, 2)
    q = lax.div(me, 2)
    partner = me + 1 - 2 * c
    count = count_ref[0]

    def remote(src, dst, a, b, dev):
        return pltpu.make_async_remote_copy(
            src_ref=src, dst_ref=dst, send_sem=a, recv_sem=b,
            device_id=dev, device_id_type=MESH,
        )

    def load(i):
        return pltpu.make_async_copy(frames_ref.at[0, pl.ds(i * H, H)], x.at[i], ld.at[i])

    for i in range(NB):
        load(i).start()

    zpeer = []
    for k in range(steps):
        bit = lax.rem(lax.div(z, 2**k), 2)
        zpeer.append(z + 2**k * (1 - 2 * bit))
    barrier = pltpu.get_barrier_semaphore()
    for k in range(1, T):
        pl.semaphore_signal(
            barrier, inc=1, device_id={"tm": lax.rem(me + k, T)}, device_id_type=MESH
        )
    for k in range(steps):
        pl.semaphore_signal(barrier, inc=1, device_id={"group": zpeer[k]}, device_id_type=MESH)
    pl.semaphore_wait(barrier, T - 1 + steps)

    def send_head():
        return remote(frames_ref.at[0, pl.ds(0, H)], head, hs.at[0], hr.at[0], {"tm": me - 1})

    def send_tail():
        return remote(frames_ref.at[0, pl.ds(R - H, H)], tail, hs.at[1], hr.at[1], {"tm": me + 1})

    @pl.when(me > 0)
    def _():
        send_head().start()

    @pl.when(me < T - 1)
    def _():
        send_tail().start()

    def put_transposed(block, base, slot):
        rows = lax.broadcasted_iota(jnp.int32, (H, 128), 0) + base
        keep = jnp.where(rows < count, 1.0, 0.0).astype(jnp.bfloat16)
        masked = block * jnp.concatenate([keep] * (F // 128), axis=1)
        xt[slot, 0:F, :] = masked.T
        cols = lax.broadcasted_iota(jnp.int32, (PAD, H), 1) + base
        xt[slot, F:, :] = jnp.where(cols < count, 1.0, 0.0).astype(jnp.bfloat16)

    def product(slot, block):
        return jnp.dot(xt[slot], block, preferred_element_type=jnp.float32)

    acc[...] = jnp.zeros_like(acc)

    def inst_step(i, carry):
        load(i).wait()
        put_transposed(x[i], me * R + i * H, i)
        acc[...] += product(i, x[i])
        return carry

    lax.fori_loop(0, NB, inst_step, 0)
    for d in range(T):
        ai[d % 2, d // 2] = acc[d * S:(d + 1) * S, :]
    sx[...] = acc[F:F + EXTRA, :]
    p1i = remote(ai.at[1 - c], r1i, s1.at[0], e1.at[0], {"tm": partner})
    p1i.start()

    acc[...] = jnp.zeros_like(acc)

    def lag_step(i, carry):
        acc[...] += product(i, x[i + LAG // H])
        return carry

    lax.fori_loop(0, NB - LAG // H, lag_step, 0)

    def spread(buf, landed, row):
        out = []
        for k in range(1, Q):
            q2 = lax.rem(q + k, Q)
            out.append(remote(
                buf.at[c, q2], landed.at[k - 1], s2.at[row, k - 1], e2.at[row, k - 1],
                {"tm": 2 * q2 + c},
            ))
        return out

    p1i.wait_recv()
    for k in range(Q):
        ai[c, k] += r1i[k]
    p2i = spread(ai, r2i, 0)
    for copy in p2i:
        copy.start()

    @pl.when(me < T - 1)
    def _():
        send_head().wait_recv()
        acc[...] += product(NB - 2, head[...])

    @pl.when(me > 0)
    def _():
        send_tail().wait_recv()
        put_transposed(tail[...], me * R - H, NB - 1)
        acc[...] += product(NB - 1, x[1])

    which = lax.broadcasted_iota(jnp.int32, (EXTRA, F), 0)
    sums = jnp.where(which < 3, sx[...], acc[F:F + EXTRA, :])
    for d in range(T):
        al[d % 2, d // 2, 0:S, :] = acc[d * S:(d + 1) * S, :]
        al[d % 2, d // 2, S:, :] = sums
    p1l = remote(al.at[1 - c], r1l, s1.at[1], e1.at[1], {"tm": partner})
    p1l.start()

    def exchange(buf, landed, k, row):
        return remote(
            buf.at[k], landed.at[k], sz.at[row, k], ez.at[row, k], {"group": zpeer[k]}
        )

    for copy in p2i:
        copy.wait_recv()
    total = ai[c, q]
    for k in range(Q - 1):
        total = total + r2i[k]
    zi[0] = total
    zi_copies = [exchange(zi, zri, k, 0) for k in range(steps)]
    zl_copies = [exchange(zl, zrl, k, 1) for k in range(steps)]
    zi_copies[0].start()

    p1l.wait_recv()
    for k in range(Q):
        al[c, k] += r1l[k]
    p2l = spread(al, r2l, 1)
    for copy in p2l:
        copy.start()

    def advance(copies, buf, landed, k):
        copies[k].wait_recv()
        buf[k + 1] = buf[k] + landed[k]
        if k + 1 < steps:
            copies[k + 1].start()

    for k in range(steps - 1):
        advance(zi_copies, zi, zri, k)

    for copy in p2l:
        copy.wait_recv()
    total = al[c, q]
    for k in range(Q - 1):
        total = total + r2l[k]
    number = count.astype(jnp.float32)
    zl[0, 0:S, :] = total[0:S]
    zl[0, S:, :] = jnp.where(which < 6, total[S:], number)
    zl_copies[0].start()

    rows = lax.broadcasted_iota(jnp.int32, (S, F), 0) + me * S
    cols = lax.broadcasted_iota(jnp.int32, (S, F), 1)

    def centred(inst, lagged, extra, out_i, out_l):
        n = extra[6:7, :]
        mx = extra[0:1, :] / n
        my = extra[3:4, :] / n
        column = jnp.sum(jnp.where(rows == cols, jnp.broadcast_to(mx, (S, F)), 0.0), axis=1, keepdims=True)
        out_i(inst / n - column * mx)
        out_l(lagged / n - column * my)

    def put(ref, lead):
        def store(v):
            if lead:
                ref[0] = v
            else:
                ref[...] = v
        return store

    centred(zi[0], zl[0, 0:S, :], zl[0, S:, :], put(gi_ref, True), put(gl_ref, True))
    advance(zi_copies, zi, zri, steps - 1)
    for k in range(steps):
        advance(zl_copies, zl, zrl, k)
    centred(
        zi[steps], zl[steps, 0:S, :], zl[steps, S:, :], put(pi_ref, False), put(po_ref, False)
    )

    @pl.when(me > 0)
    def _():
        send_head().wait_send()

    @pl.when(me < T - 1)
    def _():
        send_tail().wait_send()

    for copy in [p1i, p1l, *p2i, *p2l, *zi_copies, *zl_copies]:
        copy.wait_send()


def on_device(T, G, frames, pair_count):
    _, R, F = frames.shape
    S, Q, H = F // T, T // 2, LAG // 2
    NB = R // H
    steps = G.bit_length() - 1
    f32, bf16 = jnp.float32, jnp.bfloat16
    V, D = pltpu.VMEM, pltpu.SemaphoreType.DMA
    vmem = pl.BlockSpec(memory_space=pltpu.VMEM)
    return pl.pallas_call(
        functools.partial(kernel, T, G),
        out_shape=(
            jax.ShapeDtypeStruct((1, S, F), f32),
            jax.ShapeDtypeStruct((1, S, F), f32),
            jax.ShapeDtypeStruct((S, F), f32),
            jax.ShapeDtypeStruct((S, F), f32),
        ),
        in_specs=[pl.BlockSpec(memory_space=pltpu.SMEM), pl.BlockSpec(memory_space=pl.ANY)],
        out_specs=(vmem,) * 4,
        scratch_shapes=[
            V((NB, H, F), bf16),
            V((NB, F + PAD, H), bf16),
            V((H, F), bf16),
            V((H, F), bf16),
            V((F + PAD, F), f32),
            V((EXTRA, F), f32),
            V((2, Q, S, F), f32),
            V((2, Q, S + EXTRA, F), f32),
            V((Q, S, F), f32),
            V((Q, S + EXTRA, F), f32),
            V((Q - 1, S, F), f32),
            V((Q - 1, S + EXTRA, F), f32),
            V((steps + 1, S, F), f32),
            V((steps + 1, S + EXTRA, F), f32),
            V((steps, S, F), f32),
            V((steps, S + EXTRA, F), f32),
            D((NB,)),
            D((2,)),
            D((2,)),
            D((2,)),
            D((2,)),
            D((2, Q - 1)),
            D((2, Q - 1)),
            D((2, steps)),
            D((2, steps)),
        ],
        compiler_params=pltpu.CompilerParams(
            collective_id=0, has_side_effects=True, vmem_limit_bytes=60 * 1024 * 1024
        ),
    )(pair_count, frames)


def solution(mesh):
    in_specs = (P("group", "tm", None), P("group"))
    out_specs = (P("group", "tm", None), P("group", "tm", None), P("tm", None), P("tm", None))
    body = functools.partial(on_device, mesh.shape["tm"], mesh.shape["group"])
    return jax.shard_map(
        body, mesh=mesh, in_specs=in_specs, out_specs=out_specs, check_vma=False
    )
```

time: 151 us -> 64.3 us (0.43)
  Pallas kernels: 0 us -> 56.6 us
  waiting for transfers between devices: 55.9 us -> 0 us
  blocking collectives: 34.1 us -> 0 us
  matrix products: 20.7 us -> 0 us
  other arithmetic: 14.9 us -> 0 us
  between operations: 14.5 us -> 1.29 us
  local copies, waits for them, and re-layouts: 8.91 us -> 6.27 us
    pallas_call x0 -> x1, Pallas kernels: none -> 56.6 us  [on_device(): pl.pallas_call(functools.partial(kernel, T, G), out_shape=(jax.ShapeDtype...]
    psum x1 -> x0, waiting for transfers between devices: 35.3 us -> none  [on_device(): lax.psum((part_inst, part_lag, tot_x, tot_y, number.reshape(1)), 'group')]
    psum x2 -> x0, blocking collectives: 34.1 us -> none  [the longest x1 21.4 us: on_device(): tot_x, tot_y = lax.psum((sum_x, sum_y), 'tm')]
    dot_general x2 -> x0, matrix products: 20.7 us -> none  [the longest x1 11.5 us: on_device(): lax.dot_general(masked, local, contract, preferred_element_type=jnp.float32)]
    reduce_scatter x2 -> x0, waiting for transfers between devices: 20.6 us -> none  [the longest x1 20.6 us: on_device(): lax.psum_scatter(raw_lag, 'tm', scatter_dimension=0, tiled=True)]
    reduce_sum x1 -> x0, other arithmetic: 9.06 us -> none  [on_device(): sum_y = jnp.sum(later * weight, axis=0)]
    slice x2 -> x0, local copies, waits for them, and re-layouts: 6.26 us -> none  [the longest x1 3.19 us: on_device(): lagged = jnp.concatenate([local[LAG:], incoming], axis=0)]
    unnamed x2 -> x4, local copies, waits for them, and re-layouts: 2.64 us -> 6.27 us
  transfers between devices with their start and end apart: 4 -> 0, of which waited for: 2 -> 0; matrix products, arithmetic and copies ran while one was open for 23% -> 0% of each run, Pallas kernels for 0% -> 0%
where the time goes in v1:
time: 64.3 us; the launch traced here: 64.1 us
  Pallas kernels  56.6 us (88%)
  local copies, waits for them, and re-layouts  6.27 us (10%)
  between operations  1.29 us (2%)
    pallas_call x1, Pallas kernels, on_device(): pl.pallas_call(functools.partial(kernel, T, G), out_shape=(jax.ShapeDtype...  56.6 us
    unnamed x4, local copies, waits for them, and re-layouts  6.27 us

profile of v1, /device:TPU:0, one launch (start us, length us, event | category | flops | bytes accessed | tf_op | source)
XLA Modules:
  0.0 64.1 jit_solution(5715957311333024317)
XLA Ops:
  1.3 56.6 %shard_map.57 = (f32[1,64,512]{2,1,0:T(8,128)}, f32[1,64,512]{2,1,0:T(8,128)}, f32[64,512]{1,0:T(8,128)}, f32[64,512]{1,0:T(8,128)}) custom-call(s32[1]{0:T(128)S(6)} %copy.10.count_ref, bf16[1,8192,512]{2,1,0:T(8,128)(2,1)} %frames_ref.1), custom_call_target="tpu_custom_call" | custom-call | tf_op jit(solution)/shard_map/pallas_call | solution.py:232
  57.8 1.6 %copy.11 = f32[1,64,512]{2,1,0:T(8,128)} copy(f32[1,64,512]{2,1,0:T(8,128)} %get-tuple-element.8) | data formatting | bytes 262144
  59.4 1.6 %copy.12 = f32[1,64,512]{2,1,0:T(8,128)} copy(f32[1,64,512]{2,1,0:T(8,128)} %get-tuple-element.9) | data formatting | bytes 262144
  61.0 1.6 %copy.13 = f32[64,512]{1,0:T(8,128)} copy(f32[64,512]{1,0:T(8,128)} %get-tuple-element.10) | data formatting | bytes 262144
  62.5 1.6 %copy.14 = f32[64,512]{1,0:T(8,128)} copy(f32[64,512]{1,0:T(8,128)} %get-tuple-element.11) | data formatting | bytes 262144

commit v2 on v1

v2 whole, which is shorter than its diff:
```python
import functools

import jax
import jax.numpy as jnp
from jax import lax
from jax.experimental import pallas as pl
from jax.experimental.pallas import tpu as pltpu
from jax.sharding import PartitionSpec as P

LAG = 2048
MESH = pl.DeviceIdType.MESH
PAD = 16
EXTRA = 8
CUTS = 4
HALVES = 2


def kernel(
    T, G, count_ref, frames_ref, gi_ref, gl_ref, pi_ref, po_ref,
    x, xt, head, tail, acc, sx, ai, al, r1i, r1l, r2i, r2l, zi, zl, zri, zrl,
    ld, hs, hr, s1, e1, s2, e2, sz, ez,
):
    F = frames_ref.shape[2]
    R = frames_ref.shape[1]
    H = LAG // CUTS
    NB = R // H
    W = F // HALVES
    S = F // T
    Q = T // 2
    steps = G.bit_length() - 1
    me = lax.axis_index("tm")
    z = lax.axis_index("group")
    c = lax.rem(me, 2)
    q = lax.div(me, 2)
    partner = me + 1 - 2 * c
    count = count_ref[0]

    def remote(src, dst, a, b, dev):
        return pltpu.make_async_remote_copy(
            src_ref=src, dst_ref=dst, send_sem=a, recv_sem=b,
            device_id=dev, device_id_type=MESH,
        )

    def load(i):
        return pltpu.make_async_copy(frames_ref.at[0, pl.ds(i * H, H)], x.at[i], ld.at[i])

    for i in range(NB):
        load(i).start()

    zpeer = []
    for k in range(steps):
        bit = lax.rem(lax.div(z, 2**k), 2)
        zpeer.append(z + 2**k * (1 - 2 * bit))
    barrier = pltpu.get_barrier_semaphore()
    for k in range(1, T):
        pl.semaphore_signal(
            barrier, inc=1, device_id={"tm": lax.rem(me + k, T)}, device_id_type=MESH
        )
    for k in range(steps):
        pl.semaphore_signal(barrier, inc=1, device_id={"group": zpeer[k]}, device_id_type=MESH)
    pl.semaphore_wait(barrier, T - 1 + steps)

    def kept(b):
        if T != 8:
            return CUTS // 2
        turn = lax.rem(b, 2) * (1 - lax.rem(lax.div(b, 2), 2))
        return CUTS // 2 + turn * (2 * lax.div(b, 4) - 1)

    before = lax.rem(me + T - 1, T)

    def send_head(j):
        return remote(
            frames_ref.at[0, pl.ds(j * H, H)], head.at[j], hs.at[0, j], hr.at[0, j], {"tm": me - 1}
        )

    def send_tail(j):
        return remote(
            frames_ref.at[0, pl.ds(R - LAG + j * H, H)], tail.at[j], hs.at[1, j], hr.at[1, j],
            {"tm": me + 1},
        )

    def sent(act):
        for j in range(CUTS):
            @pl.when((me > 0) & (j < kept(before)))
            def _():
                act(send_head(j))

            @pl.when((me < T - 1) & (j >= kept(me)))
            def _():
                act(send_tail(j))

    sent(lambda copy: copy.start())

    def put_transposed(block, base, slot):
        rows = lax.broadcasted_iota(jnp.int32, (H, 128), 0) + base
        keep = jnp.where(rows < count, 1.0, 0.0).astype(jnp.bfloat16)
        masked = block * jnp.concatenate([keep] * (F // 128), axis=1)
        xt[slot, 0:F, :] = masked.T
        cols = lax.broadcasted_iota(jnp.int32, (PAD, H), 1) + base
        xt[slot, F:, :] = jnp.where(cols < count, 1.0, 0.0).astype(jnp.bfloat16)

    def product(slot, block):
        return jnp.dot(xt[slot], block, preferred_element_type=jnp.float32)

    acc[...] = jnp.zeros_like(acc)

    def inst_step(i, carry):
        for j in (2 * i, 2 * i + 1):
            load(j).wait()
            put_transposed(x[j], me * R + j * H, j)
        acc[...] += product(2 * i, x[2 * i]) + product(2 * i + 1, x[2 * i + 1])
        return carry

    lax.fori_loop(0, NB // 2, inst_step, 0)
    for d in range(T):
        ai[d % 2, d // 2] = acc[d * S:(d + 1) * S, :]
    sx[...] = acc[F:F + EXTRA, :]
    p1i = remote(ai.at[1 - c], r1i, s1.at[0], e1.at[0], {"tm": partner})
    p1i.start()

    acc[...] = jnp.zeros_like(acc)

    def lag_step(i, carry):
        j = 2 * i
        acc[...] += product(j, x[j + CUTS]) + product(j + 1, x[j + 1 + CUTS])
        return carry

    lax.fori_loop(0, (NB - CUTS) // 2, lag_step, 0)

    def spread(buf, landed, row):
        out = []
        for k in range(1, Q):
            q2 = lax.rem(q + k, Q)
            out.append(remote(
                buf.at[c, q2], landed.at[k - 1], s2.at[row, k - 1], e2.at[row, k - 1],
                {"tm": 2 * q2 + c},
            ))
        return out

    p1i.wait_recv()
    for k in range(Q):
        ai[c, k] += r1i[k]
    p2i = spread(ai, r2i, 0)
    for j in range(CUTS):
        @pl.when((me < T - 1) & (j < kept(me)))
        def _():
            send_head(j).wait_recv()

        @pl.when((me > 0) & (j >= kept(before)))
        def _():
            send_tail(j).wait_recv()
    for copy in p2i:
        copy.start()

    @pl.when(me > 0)
    def _():
        def turn_step(j, carry):
            put_transposed(tail[j], me * R - LAG + j * H, j)
            return carry

        lax.fori_loop(kept(before), CUTS, turn_step, 0)

    which = lax.broadcasted_iota(jnp.int32, (EXTRA, W), 0)
    p1l = []
    for h in range(HALVES):
        cols = slice(h * W, (h + 1) * W)

        @pl.when(me < T - 1)
        def _():
            def head_step(j, carry):
                acc[:, cols] += product(NB - CUTS + j, head[j, :, cols])
                return carry

            lax.fori_loop(0, kept(me), head_step, 0)

        @pl.when(me > 0)
        def _():
            def tail_step(j, carry):
                acc[:, cols] += product(j, x[j, :, cols])
                return carry

            lax.fori_loop(kept(before), CUTS, tail_step, 0)

        sums = jnp.where(which < 3, sx[:, cols], acc[F:F + EXTRA, cols])
        for d in range(T):
            al[h, d % 2, d // 2, 0:S, :] = acc[d * S:(d + 1) * S, cols]
            al[h, d % 2, d // 2, S:, :] = sums
        p1l.append(remote(al.at[h, 1 - c], r1l.at[h], s1.at[1 + h], e1.at[1 + h], {"tm": partner}))
        p1l[h].start()

    def exchange(buf, landed, k, row):
        return remote(
            buf.at[k], landed.at[k], sz.at[row, k], ez.at[row, k], {"group": zpeer[k]}
        )

    p2l = []
    for h in range(HALVES):
        p1l[h].wait_recv()
        for k in range(Q):
            al[h, c, k] += r1l[h, k]
        p2l.append(spread(al.at[h], r2l.at[h], 1 + h))
        for copy in p2l[h]:
            copy.start()

    for copy in p2i:
        copy.wait_recv()
    total = ai[c, q]
    for k in range(Q - 1):
        total = total + r2i[k]
    zi[0] = total
    zi_copies = [exchange(zi, zri, k, 0) for k in range(steps)]
    zl_copies = [
        [exchange(zl.at[h], zrl.at[h], k, 1 + h) for k in range(steps)] for h in range(HALVES)
    ]
    zi_copies[0].start()

    def advance(copies, buf, landed, k):
        copies[k].wait_recv()
        buf[k + 1] = buf[k] + landed[k]
        if k + 1 < steps:
            copies[k + 1].start()

    for k in range(steps - 1):
        advance(zi_copies, zi, zri, k)

    number = count.astype(jnp.float32)
    for h in range(HALVES):
        for copy in p2l[h]:
            copy.wait_recv()
        total = al[h, c, q]
        for k in range(Q - 1):
            total = total + r2l[h, k]
        zl[h, 0, 0:S, :] = total[0:S]
        zl[h, 0, S:, :] = jnp.where(which < 6, total[S:], number)
        zl_copies[h][0].start()

    def lagged(k):
        return jnp.concatenate([zl[h, k] for h in range(HALVES)], axis=1)

    rows = lax.broadcasted_iota(jnp.int32, (S, F), 0) + me * S
    cols = lax.broadcasted_iota(jnp.int32, (S, F), 1)

    def centred(inst, both, out_i, out_l):
        extra = both[S:]
        n = extra[6:7, :]
        mx = extra[0:1, :] / n
        my = extra[3:4, :] / n
        wide = jnp.where(rows == cols, jnp.broadcast_to(mx, (S, F)), 0.0)
        column = jnp.sum(wide, axis=1, keepdims=True)
        out_i(inst / n - column * mx)
        out_l(both[0:S] / n - column * my)

    def put(ref, lead):
        def store(v):
            if lead:
                ref[0] = v
            else:
                ref[...] = v
        return store

    centred(zi[0], lagged(0), put(gi_ref, True), put(gl_ref, True))
    advance(zi_copies, zi, zri, steps - 1)
    for k in range(steps):
        for h in range(HALVES):
            advance(zl_copies[h], zl.at[h], zrl.at[h], k)
    centred(zi[steps], lagged(steps), put(pi_ref, False), put(po_ref, False))

    sent(lambda copy: copy.wait_send())
    for group in [[p1i], p1l, p2i, *p2l, zi_copies, *zl_copies]:
        for copy in group:
            copy.wait_send()


def on_device(T, G, frames, pair_count):
    _, R, F = frames.shape
    S, Q, H, W = F // T, T // 2, LAG // CUTS, F // HALVES
    NB = R // H
    steps = G.bit_length() - 1
    f32, bf16 = jnp.float32, jnp.bfloat16
    V, D = pltpu.VMEM, pltpu.SemaphoreType.DMA
    vmem = pl.BlockSpec(memory_space=pltpu.VMEM)
    return pl.pallas_call(
        functools.partial(kernel, T, G),
        out_shape=(
            jax.ShapeDtypeStruct((1, S, F), f32),
            jax.ShapeDtypeStruct((1, S, F), f32),
            jax.ShapeDtypeStruct((S, F), f32),
            jax.ShapeDtypeStruct((S, F), f32),
        ),
        in_specs=[pl.BlockSpec(memory_space=pltpu.SMEM), pl.BlockSpec(memory_space=pl.ANY)],
        out_specs=(vmem,) * 4,
        scratch_shapes=[
            V((NB, H, F), bf16),
            V((NB, F + PAD, H), bf16),
            V((CUTS, H, F), bf16),
            V((CUTS, H, F), bf16),
            V((F + PAD, F), f32),
            V((EXTRA, F), f32),
            V((2, Q, S, F), f32),
            V((HALVES, 2, Q, S + EXTRA, W), f32),
            V((Q, S, F), f32),
            V((HALVES, Q, S + EXTRA, W), f32),
            V((Q - 1, S, F), f32),
            V((HALVES, Q - 1, S + EXTRA, W), f32),
            V((steps + 1, S, F), f32),
            V((HALVES, steps + 1, S + EXTRA, W), f32),
            V((steps, S, F), f32),
            V((HALVES, steps, S + EXTRA, W), f32),
            D((NB,)),
            D((2, CUTS)),
            D((2, CUTS)),
            D((1 + HALVES,)),
            D((1 + HALVES,)),
            D((1 + HALVES, Q - 1)),
            D((1 + HALVES, Q - 1)),
            D((1 + HALVES, steps)),
            D((1 + HALVES, steps)),
        ],
        compiler_params=pltpu.CompilerParams(
            collective_id=0, has_side_effects=True, vmem_limit_bytes=60 * 1024 * 1024
        ),
    )(pair_count, frames)


def solution(mesh):
    in_specs = (P("group", "tm", None), P("group"))
    out_specs = (P("group", "tm", None), P("group", "tm", None), P("tm", None), P("tm", None))
    body = functools.partial(on_device, mesh.shape["tm"], mesh.shape["group"])
    return jax.shard_map(
        body, mesh=mesh, in_specs=in_specs, out_specs=out_specs, check_vma=False
    )
```

time: 64.3 us -> 63.3 us (0.984)
  Pallas kernels: 56.6 us -> 55.6 us
    pallas_call x1, Pallas kernels: 56.6 us -> 55.6 us  [on_device(): pl.pallas_call(functools.partial(kernel, T, G), out_shape=(jax.ShapeDtype...]
where the time goes in v2:
time: 63.3 us; the launch traced here: 63.1 us
  Pallas kernels  55.6 us (88%)
  local copies, waits for them, and re-layouts  6.27 us (10%)
  between operations  1.29 us (2%)
    pallas_call x1, Pallas kernels, on_device(): pl.pallas_call(functools.partial(kernel, T, G), out_shape=(jax.ShapeDtype...  55.6 us
    unnamed x4, local copies, waits for them, and re-layouts  6.27 us

profile of v2, /device:TPU:0, one launch (start us, length us, event | category | flops | bytes accessed | tf_op | source)
XLA Modules:
  0.0 63.1 jit_solution(3377589577402815549)
XLA Ops:
  1.3 55.6 %shard_map.57 = (f32[1,64,512]{2,1,0:T(8,128)}, f32[1,64,512]{2,1,0:T(8,128)}, f32[64,512]{1,0:T(8,128)}, f32[64,512]{1,0:T(8,128)}) custom-call(s32[1]{0:T(128)S(6)} %copy.10.count_ref, bf16[1,8192,512]{2,1,0:T(8,128)(2,1)} %frames_ref.1), custom_call_target="tpu_custom_call" | custom-call | tf_op jit(solution)/shard_map/pallas_call | solution.py:282
  56.8 1.6 %copy.11 = f32[1,64,512]{2,1,0:T(8,128)} copy(f32[1,64,512]{2,1,0:T(8,128)} %get-tuple-element.8) | data formatting | bytes 262144
  58.4 1.6 %copy.12 = f32[1,64,512]{2,1,0:T(8,128)} copy(f32[1,64,512]{2,1,0:T(8,128)} %get-tuple-element.9) | data formatting | bytes 262144
  60.0 1.6 %copy.13 = f32[64,512]{1,0:T(8,128)} copy(f32[64,512]{1,0:T(8,128)} %get-tuple-element.10) | data formatting | bytes 262144
  61.5 1.6 %copy.14 = f32[64,512]{1,0:T(8,128)} copy(f32[64,512]{1,0:T(8,128)} %get-tuple-element.11) | data formatting | bytes 262144

commit v3 on v2

--- a/solution.py
+++ b/solution.py
@@ -16,7 +16,7 @@
 
 
 def kernel(
-    T, G, count_ref, frames_ref, gi_ref, gl_ref, pi_ref, po_ref,
+    T, G, count_ref, frames_ref, own_ref, all_ref,
     x, xt, head, tail, acc, sx, ai, al, r1i, r1l, r2i, r2l, zi, zl, zri, zrl,
     ld, hs, hr, s1, e1, s2, e2, sz, ez,
 ):
@@ -234,41 +234,36 @@
         zl[h, 0, S:, :] = jnp.where(which < 6, total[S:], number)
         zl_copies[h][0].start()
 
-    def lagged(k):
-        return jnp.concatenate([zl[h, k] for h in range(HALVES)], axis=1)
-
-    rows = lax.broadcasted_iota(jnp.int32, (S, F), 0) + me * S
-    cols = lax.broadcasted_iota(jnp.int32, (S, F), 1)
-
-    def centred(inst, both, out_i, out_l):
-        extra = both[S:]
-        n = extra[6:7, :]
-        mx = extra[0:1, :] / n
-        my = extra[3:4, :] / n
-        wide = jnp.where(rows == cols, jnp.broadcast_to(mx, (S, F)), 0.0)
-        column = jnp.sum(wide, axis=1, keepdims=True)
-        out_i(inst / n - column * mx)
-        out_l(both[0:S] / n - column * my)
-
-    def put(ref, lead):
-        def store(v):
-            if lead:
-                ref[0] = v
-            else:
-                ref[...] = v
-        return store
-
-    centred(zi[0], lagged(0), put(gi_ref, True), put(gl_ref, True))
+    def out(ref, k):
+        ref[0:S, :] = zi[k]
+        for h in range(HALVES):
+            ref[S:, h * W:(h + 1) * W] = zl[h, k]
+
+    out(own_ref, 0)
     advance(zi_copies, zi, zri, steps - 1)
     for k in range(steps):
         for h in range(HALVES):
             advance(zl_copies[h], zl.at[h], zrl.at[h], k)
-    centred(zi[steps], lagged(steps), put(pi_ref, False), put(po_ref, False))
+    out(all_ref, steps)
 
     sent(lambda copy: copy.wait_send())
     for group in [[p1i], p1l, p2i, *p2l, zi_copies, *zl_copies]:
         for copy in group:
             copy.wait_send()
+
+
+def centre(own_ref, all_ref, gi_ref, gl_ref, pi_ref, po_ref):
+    S, F = pi_ref.shape
+    rows = lax.broadcasted_iota(jnp.int32, (S, F), 0) + lax.axis_index("tm") * S
+    cols = lax.broadcasted_iota(jnp.int32, (S, F), 1)
+    for ref, out_i, out_l in ((own_ref, gi_ref.at[0], gl_ref.at[0]), (all_ref, pi_ref, po_ref)):
+        n = ref[2 * S + 6:2 * S + 7, :]
+        mx = ref[2 * S:2 * S + 1, :] / n
+        my = ref[2 * S + 3:2 * S + 4, :] / n
+        wide = jnp.where(rows == cols, jnp.broadcast_to(mx, (S, F)), 0.0)
+        column = jnp.sum(wide, axis=1, keepdims=True)
+        out_i[...] = ref[0:S, :] / n - column * mx
+        out_l[...] = ref[S:2 * S, :] / n - column * my
 
 
 def on_device(T, G, frames, pair_count):
@@ -279,16 +274,11 @@
     f32, bf16 = jnp.float32, jnp.bfloat16
     V, D = pltpu.VMEM, pltpu.SemaphoreType.DMA
     vmem = pl.BlockSpec(memory_space=pltpu.VMEM)
-    return pl.pallas_call(
+    own, whole = pl.pallas_call(
         functools.partial(kernel, T, G),
-        out_shape=(
-            jax.ShapeDtypeStruct((1, S, F), f32),
-            jax.ShapeDtypeStruct((1, S, F), f32),
-            jax.ShapeDtypeStruct((S, F), f32),
-            jax.ShapeDtypeStruct((S, F), f32),
-        ),
+        out_shape=(jax.ShapeDtypeStruct((2 * S + EXTRA, F), f32),) * 2,
         in_specs=[pl.BlockSpec(memory_space=pltpu.SMEM), pl.BlockSpec(memory_space=pl.ANY)],
-        out_specs=(vmem,) * 4,
+        out_specs=(vmem,) * 2,
         scratch_shapes=[
             V((NB, H, F), bf16),
             V((NB, F + PAD, H), bf16),
@@ -317,9 +307,21 @@
             D((1 + HALVES, steps)),
         ],
         compiler_params=pltpu.CompilerParams(
-            collective_id=0, has_side_effects=True, vmem_limit_bytes=60 * 1024 * 1024
+            collective_id=0, has_side_effects=True, vmem_limit_bytes=48 * 1024 * 1024
         ),
     )(pair_count, frames)
+    return pl.pallas_call(
+        centre,
+        out_shape=(
+            jax.ShapeDtypeStruct((1, S, F), f32),
+            jax.ShapeDtypeStruct((1, S, F), f32),
+            jax.ShapeDtypeStruct((S, F), f32),
+            jax.ShapeDtypeStruct((S, F), f32),
+        ),
+        in_specs=[vmem, vmem],
+        out_specs=(vmem,) * 4,
+        compiler_params=pltpu.CompilerParams(vmem_limit_bytes=4 * 1024 * 1024),
+    )(own, whole)
 
 
 def solution(mesh):

time: 63.3 us -> 57.1 us (0.902)
  local copies, waits for them, and re-layouts: 6.27 us -> 0 us
    unnamed x4 -> x0, local copies, waits for them, and re-layouts: 6.27 us -> none
    pallas_call x0 -> x1, Pallas kernels: none -> 0.9 us  [on_device(): pl.pallas_call(centre, out_shape=(jax.ShapeDtypeStruct((1, S, F), f32), j...]
    pallas_call x1, Pallas kernels: 55.6 us -> 54.7 us  [on_device(): pl.pallas_call(functools.partial(kernel, T, G), out_shape=(jax.ShapeDtype...]
where the time goes in v3:
time: 57.1 us; the launch traced here: 56.9 us
  Pallas kernels  55.6 us (97%)
  between operations  1.28 us (2%)
    pallas_call x1, Pallas kernels, on_device(): pl.pallas_call(functools.partial(kernel, T, G), out_shape=(jax.ShapeDtype...  54.7 us

profile of v3, /device:TPU:0, one launch (start us, length us, event | category | flops | bytes accessed | tf_op | source)
XLA Modules:
  0.0 56.9 jit_solution(4911924184527069665)
XLA Ops:
  1.3 54.7 %shard_map.57 = (f32[136,512]{1,0:T(8,128)S(1)}, f32[136,512]{1,0:T(8,128)S(1)}) custom-call(s32[1]{0:T(128)S(6)} %copy.6.count_ref, bf16[1,8192,512]{2,1,0:T(8,128)(2,1)} %frames_ref.1), custom_call_target="tpu_custom_call" | custom-call | tf_op jit(solution)/shard_map/pallas_call | solution.py:277
  56.0 0.9 %shard_map.58 = (f32[1,64,512]{2,1,0:T(8,128)}, f32[1,64,512]{2,1,0:T(8,128)}, f32[64,512]{1,0:T(8,128)}, f32[64,512]{1,0:T(8,128)}) custom-call(f32[136,512]{1,0:T(8,128)S(1)} %get-tuple-element.6.own_ref, f32[136,512]{1,0:T(8,128)S(1)} %get-tuple-element.7.all_ref), custom_call_target="tpu_custom_call" | custom-call | tf_op jit(solution)/shard_map/pallas_call | solution.py:313

commit v4 on v3

--- a/solution.py
+++ b/solution.py
@@ -18,7 +18,7 @@
 def kernel(
     T, G, count_ref, frames_ref, own_ref, all_ref,
     x, xt, head, tail, acc, sx, ai, al, r1i, r1l, r2i, r2l, zi, zl, zri, zrl,
-    ld, hs, hr, s1, e1, s2, e2, sz, ez,
+    ld, hs, hr, s1, e1, s2, e2, sz, ez, sf,
 ):
     F = frames_ref.shape[2]
     R = frames_ref.shape[1]
@@ -51,6 +51,11 @@
     for k in range(steps):
         bit = lax.rem(lax.div(z, 2**k), 2)
         zpeer.append(z + 2**k * (1 - 2 * bit))
+    relay = G == 4
+    if relay:
+        inner = lax.div(z + 1, 2) == 1
+        outer = z + 2 * lax.div(z, 2) - 1
+        zpeer[1] = 3 - z
     barrier = pltpu.get_barrier_semaphore()
     for k in range(1, T):
         pl.semaphore_signal(
@@ -140,47 +145,46 @@
     p1i.wait_recv()
     for k in range(Q):
         ai[c, k] += r1i[k]
-    p2i = spread(ai, r2i, 0)
-    for j in range(CUTS):
-        @pl.when((me < T - 1) & (j < kept(me)))
-        def _():
+    square = Q == 4
+    if square:
+        side, level = lax.rem(q, 2), lax.div(q, 2)
+        across = q + 1 - 2 * side
+        over = remote(
+            ai.at[c, pl.ds(2 - 2 * level, 2)], r2i.at[pl.ds(0, 2)], s2.at[0, 0], e2.at[0, 0],
+            {"tm": 2 * lax.rem(q + 2, Q) + c},
+        )
+        over.start()
+        p2i = [remote(
+            ai.at[c, across], r2i.at[2], s2.at[0, 1], e2.at[0, 1], {"tm": 2 * across + c}
+        )]
+    else:
+        p2i = spread(ai, r2i, 0)
+
+    def heads():
+        def head_step(j, carry):
             send_head(j).wait_recv()
-
-        @pl.when((me > 0) & (j >= kept(before)))
-        def _():
+            acc[...] += product(NB - CUTS + j, head[j])
+            return carry
+
+        lax.fori_loop(0, kept(me), head_step, 0)
+
+    def tails():
+        def tail_step(j, carry):
             send_tail(j).wait_recv()
-    for copy in p2i:
-        copy.start()
-
-    @pl.when(me > 0)
-    def _():
-        def turn_step(j, carry):
             put_transposed(tail[j], me * R - LAG + j * H, j)
+            acc[...] += product(j, x[j])
             return carry
 
-        lax.fori_loop(kept(before), CUTS, turn_step, 0)
+        lax.fori_loop(kept(before), CUTS, tail_step, 0)
+
+    pl.when((me < T - 1) & (c == 0))(heads)
+    pl.when(me > 0)(tails)
+    pl.when((me < T - 1) & (c == 1))(heads)
 
     which = lax.broadcasted_iota(jnp.int32, (EXTRA, W), 0)
     p1l = []
     for h in range(HALVES):
         cols = slice(h * W, (h + 1) * W)
-
-        @pl.when(me < T - 1)
-        def _():
-            def head_step(j, carry):
-                acc[:, cols] += product(NB - CUTS + j, head[j, :, cols])
-                return carry
-
-            lax.fori_loop(0, kept(me), head_step, 0)
-
-        @pl.when(me > 0)
-        def _():
-            def tail_step(j, carry):
-                acc[:, cols] += product(j, x[j, :, cols])
-                return carry
-
-            lax.fori_loop(kept(before), CUTS, tail_step, 0)
-
         sums = jnp.where(which < 3, sx[:, cols], acc[F:F + EXTRA, cols])
         for d in range(T):
             al[h, d % 2, d // 2, 0:S, :] = acc[d * S:(d + 1) * S, cols]
@@ -188,7 +192,43 @@
         p1l.append(remote(al.at[h, 1 - c], r1l.at[h], s1.at[1 + h], e1.at[1 + h], {"tm": partner}))
         p1l[h].start()
 
+    if square:
+        over.wait_recv()
+        for k in range(2):
+            ai[c, 2 * level + k] += r2i[k]
+    for copy in p2i:
+        copy.start()
+
+    class Far:
+        def __init__(self, buf, landed, row):
+            self.swap = remote(
+                buf.at[1], landed.at[1], sz.at[row, 1], ez.at[row, 1], {"group": zpeer[1]}
+            )
+            self.onward = remote(
+                landed.at[1], landed.at[1], sf.at[row], ez.at[row, 1], {"group": outer}
+            )
+
+        def start(self):
+            @pl.when(inner)
+            def _():
+                self.swap.start()
+
+        def wait_recv(self):
+            self.swap.wait_recv()
+
+            @pl.when(inner)
+            def _():
+                self.onward.start()
+
+        def wait_send(self):
+            @pl.when(inner)
+            def _():
+                self.swap.wait_send()
+                self.onward.wait_send()
+
     def exchange(buf, landed, k, row):
+        if relay and k == 1:
+            return Far(buf, landed, row)
         return remote(
             buf.at[k], landed.at[k], sz.at[row, k], ez.at[row, k], {"group": zpeer[k]}
         )
@@ -205,7 +245,7 @@
     for copy in p2i:
         copy.wait_recv()
     total = ai[c, q]
-    for k in range(Q - 1):
+    for k in range(2 if square else 0, Q - 1):
         total = total + r2i[k]
     zi[0] = total
     zi_copies = [exchange(zi, zri, k, 0) for k in range(steps)]
@@ -247,6 +287,8 @@
     out(all_ref, steps)
 
     sent(lambda copy: copy.wait_send())
+    if square:
+        over.wait_send()
     for group in [[p1i], p1l, p2i, *p2l, zi_copies, *zl_copies]:
         for copy in group:
             copy.wait_send()
@@ -305,6 +347,7 @@
             D((1 + HALVES, Q - 1)),
             D((1 + HALVES, steps)),
             D((1 + HALVES, steps)),
+            D((1 + HALVES,)),
         ],
         compiler_params=pltpu.CompilerParams(
             collective_id=0, has_side_effects=True, vmem_limit_bytes=48 * 1024 * 1024

time: 57.1 us -> 55.3 us (0.968)
  Pallas kernels: 55.6 us -> 53.9 us
    pallas_call x1, Pallas kernels: 54.7 us -> 53 us  [on_device(): pl.pallas_call(functools.partial(kernel, T, G), out_shape=(jax.ShapeDtype...]
where the time goes in v4:
time: 55.3 us; the launch traced here: 55.2 us
  Pallas kernels  53.9 us (97%)
  between operations  1.28 us (2%)
    pallas_call x1, Pallas kernels, on_device(): pl.pallas_call(functools.partial(kernel, T, G), out_shape=(jax.ShapeDtype...  53 us

profile of v4, /device:TPU:0, one launch (start us, length us, event | category | flops | bytes accessed | tf_op | source)
XLA Modules:
  0.0 55.2 jit_solution(12501048998867823214)
XLA Ops:
  1.3 53.0 %shard_map.57 = (f32[136,512]{1,0:T(8,128)S(1)}, f32[136,512]{1,0:T(8,128)S(1)}) custom-call(s32[1]{0:T(128)S(6)} %copy.6.count_ref, bf16[1,8192,512]{2,1,0:T(8,128)(2,1)} %frames_ref.1), custom_call_target="tpu_custom_call" | custom-call | tf_op jit(solution)/shard_map/pallas_call | solution.py:319
  54.3 0.9 %shard_map.58 = (f32[1,64,512]{2,1,0:T(8,128)}, f32[1,64,512]{2,1,0:T(8,128)}, f32[64,512]{1,0:T(8,128)}, f32[64,512]{1,0:T(8,128)}) custom-call(f32[136,512]{1,0:T(8,128)S(1)} %get-tuple-element.6.own_ref, f32[136,512]{1,0:T(8,128)S(1)} %get-tuple-element.7.all_ref), custom_call_target="tpu_custom_call" | custom-call | tf_op jit(solution)/shard_map/pallas_call | solution.py:356
